TPU v7x, 32 devices: a whole 2x2x4 slice. The times are simulated.
32 devices in a mesh: mem: 8 (over z, core), pat: 4 (over y, x).
Axes of the slice: x: 2, y: 2, z: 4, core: 2. Of those that a mesh axis runs over, the one named last changes fastest.
Arguments:
- background_realisations: bfloat16 [256, 8, 4, 512], P('mem', None, 'pat'), may hold values from -6 to 6
- sensed_spreads: bfloat16 [8, 4, 512, 256], P('mem', 'pat'), may hold values from -33 to 33
- departure_vector: bfloat16 [8, 4, 512], P('mem', 'pat'), may hold values from -6 to 6
- measurement_weights: bfloat16 [8, 4, 512], P('mem', 'pat'), may hold values from 0.099609375 to 10
- adjacent_tile_labels: int32 [8, 4, 9], P('mem', 'pat'), may hold values from 0 to 8, as said below
- active_lengths: int32 [8, 4], P('mem', 'pat'), may hold values from 1 to 9, as said below
Outputs:
- analysis: bfloat16 [256, 8, 4, 512], P('mem', None, 'pat')
Inputs may be any that keep to these rules, and one draw needn't show every extreme that they name: `adjacent_tile_labels`: in each patch's list the 9 codes are distinct; every code among the first active_lengths entries names a block inside the 8 patch rows. `active_lengths`: some patch uses all 9 blocks in every draw.
All inputs are finite; a program needn't handle non-finite values.
Results may differ from a plain program's by a relative error of at most 0.011.
Values may be sent and summed in bfloat16 or wider, within the bound.
A program may use at most 64 MiB of HBM per device.

v0:
```python
import jax
import jax.numpy as jnp
from jax import lax
from jax.sharding import PartitionSpec as P

ITERS = 12


def padded(block, sides, width, periodic):
    for axis, dim in sides:
        count = lax.axis_size(axis)
        forward = [(i, i + 1) for i in range(count - 1)]
        if periodic:
            forward.append((count - 1, 0))
        backward = [(target, source) for source, target in forward]
        low = lax.ppermute(
            lax.slice_in_dim(block, block.shape[dim] - width, None, axis=dim), axis, forward
        )
        high = lax.ppermute(lax.slice_in_dim(block, 0, width, axis=dim), axis, backward)
        block = jnp.concatenate([low, block, high], axis=dim)
    return block


def transform(gram, drive):
    trajectory_vectors = gram.shape[-1]
    identity = jnp.eye(trajectory_vectors, dtype=jnp.float32)[None, :, :]
    system = (trajectory_vectors - 1.0) * identity + gram
    frobenius = jnp.sqrt(jnp.sum(system * system, axis=(1, 2)))[:, None, None]
    iterate = system / frobenius
    inverse_root = identity
    for sweep in range(ITERS):
        product = jnp.einsum("pij,pjk->pik", inverse_root, iterate, precision=lax.Precision.HIGHEST)
        correction = 1.5 * identity - 0.5 * product
        iterate = jnp.einsum("pij,pjk->pik", iterate, correction, precision=lax.Precision.HIGHEST)
        inverse_root = jnp.einsum(
            "pij,pjk->pik", correction, inverse_root, precision=lax.Precision.HIGHEST
        )
    spread_part = inverse_root * jnp.sqrt((trajectory_vectors - 1.0) / frobenius)
    inner = jnp.einsum("pij,pj->pi", inverse_root, drive, precision=lax.Precision.HIGHEST)
    mean_part = (
        jnp.einsum("pij,pj->pi", inverse_root, inner, precision=lax.Precision.HIGHEST)
        / frobenius[:, :, 0]
    )
    return spread_part + mean_part[:, :, None]


def on_device(
    background_realisations,
    sensed_spreads,
    departure_vector,
    measurement_weights,
    adjacent_tile_labels,
    active_lengths,
):
    trajectory_vectors = lax.all_to_all(
        background_realisations, "mem", split_axis=1, concat_axis=0, tiled=True
    )
    column_ens, column_innov, column_rinv = (
        padded(sensed_spreads, (("pat", 1),), 1, True),
        padded(departure_vector, (("pat", 1),), 1, True),
        padded(measurement_weights, (("pat", 1),), 1, True),
    )
    window_ens, window_innov, window_rinv = (
        padded(column_ens, (("mem", 0),), 1, False),
        padded(column_innov, (("mem", 0),), 1, False),
        padded(column_rinv, (("mem", 0),), 1, False),
    )
    ens_count, rows, cols, state_len = trajectory_vectors.shape
    obs_count = sensed_spreads.shape[2]
    neighbours = adjacent_tile_labels.shape[2]
    patches = rows * cols
    width = cols + 2
    flat_ens = window_ens.reshape((rows + 2) * width, obs_count, ens_count)
    flat_innov = window_innov.reshape((rows + 2) * width, obs_count)
    flat_rinv = window_rinv.reshape((rows + 2) * width, obs_count)
    row_index = lax.broadcasted_iota(jnp.int32, (rows, cols, 1), 0)
    col_index = lax.broadcasted_iota(jnp.int32, (rows, cols, 1), 1)
    shift_row = adjacent_tile_labels // 3 - 1
    shift_col = adjacent_tile_labels % 3 - 1
    source = ((row_index + 1 + shift_row) * width + col_index + 1 + shift_col).reshape(
        patches, neighbours
    )
    slot_index = lax.broadcasted_iota(jnp.int32, (1, 1, neighbours), 2)
    live = (slot_index < active_lengths[:, :, None]).astype(jnp.float32)
    taper = (
        jnp.exp(-0.5 * (shift_row * shift_row + shift_col * shift_col).astype(jnp.float32)) * live
    ).reshape(patches, neighbours)
    blocks = flat_ens[source]
    weight = flat_rinv[source].astype(jnp.float32) * taper[:, :, None]
    scaled = (blocks * weight[:, :, :, None]).astype(jnp.bfloat16)
    weighted_innov = (weight * flat_innov[source].astype(jnp.float32)).astype(jnp.bfloat16)
    gram_part = lax.dot_general(
        scaled, blocks, (((1, 2), (1, 2)), ((0,), (0,))), preferred_element_type=jnp.float32
    )
    drive_part = lax.dot_general(
        weighted_innov, blocks, (((1, 2), (1, 2)), ((0,), (0,))), preferred_element_type=jnp.float32
    )
    mixing = transform(gram_part, drive_part).astype(jnp.bfloat16)
    values = trajectory_vectors.reshape(ens_count, patches, state_len).astype(jnp.float32)
    center = jnp.mean(values, axis=0)
    anomaly = (values - center[None, :, :]).astype(jnp.bfloat16)
    mixed = jnp.einsum("kps,pki->ips", anomaly, mixing, preferred_element_type=jnp.float32)
    analysed = (
        (center[None, :, :] + mixed).astype(jnp.bfloat16).reshape(ens_count, rows, cols, state_len)
    )
    return lax.all_to_all(analysed, "mem", split_axis=0, concat_axis=1, tiled=True)


def solution(mesh):
    placed = (
        P("mem", None, "pat", None),
        P("mem", "pat", None, None),
        P("mem", "pat", None),
        P("mem", "pat", None),
        P("mem", "pat", None),
        P("mem", "pat"),
    )
    return jax.shard_map(
        on_device,
        mesh=mesh,
        in_specs=placed,
        out_specs=P("mem", None, "pat", None),
        check_vma=False,
    )
```

profile of v0, /device:TPU:1, one launch (start us, length us, event | category | flops | bytes accessed | tf_op | source)
XLA Modules:
  0.0 89.1 jit_solution(16215473152990144531)
XLA Ops:
  0.0 2.0 %collective-permute-start.4 = (bf16[1,1,512]{2,1,0:T(2,128)(2,1)}, bf16[1,1,512]{2,1,0:T(2,128)(2,1)S(1)}, u32[]{:S(2)}, u32[]{:S(2)}) collective-permute-start(bf16[1,1,512]{2,1,0:T(2,128)(2,1)} %param.9), channel_id=1, source_target_pairs={{0,1},{1,2},{2,3},{3,0},{4,5},{5,6},{6,7},{7,4},{8,9},{9,10},{10,1... | collective-permute-start | bytes 3080 | tf_op jit(solution)/shard_map/ppermute | solution.py:16
  2.0 1.0 %collective-permute-start.5 = (bf16[1,1,512]{2,1,0:T(2,128)(2,1)}, bf16[1,1,512]{2,1,0:T(2,128)(2,1)S(1)}, u32[]{:S(2)}, u32[]{:S(2)}) collective-permute-start(bf16[1,1,512]{2,1,0:T(2,128)(2,1)} %param.9), channel_id=1, source_target_pairs={{1,0},{2,1},{3,2},{0,3},{5,4},{6,5},{7,6},{4,7},{9,8},{10,9},{11,1... | collective-permute-start | bytes 3080 | tf_op jit(solution)/shard_map/ppermute | solution.py:19
  3.0 0.5 collective-permute-start
  3.5 1.9 %collective-permute-start.1 = (bf16[1,1,512,256]{3,2,1,0:T(8,128)(2,1)}, bf16[1,1,512,256]{3,2,1,0:T(8,128)(2,1)S(1)}, u32[]{:S(2)}, u32[]{:S(2)}) collective-permute-start(bf16[1,1,512,256]{3,2,1,0:T(8,128)(2,1)} %param.7), channel_id=1, source_target_pairs={{1,0},{2,1},{3,2},{0,3},{5,4},{6,5},{7,6},{4,7},{9,8},{10,9},{11,1... | collective-permute-start | bytes 786440 | tf_op jit(solution)/shard_map/ppermute | solution.py:19
  5.6 1.7 %copy.23 = bf16[32,8,1,512]{3,0,2,1:T(8,128)(2,1)} copy(bf16[32,8,1,512]{3,1,2,0:T(8,128)(2,1)} %param.6) | data formatting | bytes 524288 | tf_op args[0]
  7.3 6.7 %all-to-all-start = ((bf16[32,8,1,512]{3,0,2,1:T(8,128)(2,1)}), bf16[32,8,1,512]{3,0,2,1:T(8,128)(2,1)S(1)}, u32[]{:S(2)}, u32[]{:S(2)}) async-start(bf16[32,8,1,512]{3,0,2,1:T(8,128)(2,1)} %copy.23), calls=%async_computation | async-start | bytes 524288 | tf_op jit(solution)/shard_map/all_to_all | solution.py:55
  14.7 0.7 fusion.25
  15.3 0.7 fusion.26
  16.0 2.6 %collective-permute-start.9 = (bf16[1,1,512]{2,1,0:T(2,128)(2,1)}, bf16[1,1,512]{2,1,0:T(2,128)(2,1)S(1)}, u32[]{:S(2)}, u32[]{:S(2)}) collective-permute-start(bf16[1,1,512]{2,1,0:T(2,128)(2,1)} %param.8), channel_id=1, source_target_pairs={{1,0},{2,1},{3,2},{0,3},{5,4},{6,5},{7,6},{4,7},{9,8},{10,9},{11,1... | collective-permute-start | bytes 3080 | tf_op jit(solution)/shard_map/ppermute | solution.py:19
  18.7 0.7 pad_maximum_fusion.3
  19.4 3.8 %collective-permute-start.6 = (bf16[1,3,512]{2,1,0:T(4,128)(2,1)S(1)}, bf16[1,3,512]{2,1,0:T(4,128)(2,1)S(1)}, u32[]{:S(2)}, u32[]{:S(2)}) collective-permute-start(bf16[1,3,512]{2,1,0:T(4,128)(2,1)S(1)} %pad_maximum_fusion.3), channel_id=1, source_target_pairs={{0,4},{4,8},{8,12},{12,16},{16,20},{20,24},{24,28},{1,5},{5,9},{9,... | collective-permute-start | bytes 9224 | tf_op jit(solution)/shard_map/ppermute | solution.py:16
  23.2 1.9 %collective-permute-start.7 = (bf16[1,3,512]{2,1,0:T(4,128)(2,1)S(1)}, bf16[1,3,512]{2,1,0:T(4,128)(2,1)S(1)}, u32[]{:S(2)}, u32[]{:S(2)}) collective-permute-start(bf16[1,3,512]{2,1,0:T(4,128)(2,1)S(1)} %pad_maximum_fusion.3), channel_id=1, source_target_pairs={{4,0},{8,4},{12,8},{16,12},{20,16},{24,20},{28,24},{5,1},{9,5},{13... | collective-permute-start | bytes 9224 | tf_op jit(solution)/shard_map/ppermute | solution.py:19
  25.2 0.7 pad_maximum_fusion.4
  25.9 3.6 %collective-permute-start.10 = (bf16[1,3,512]{2,1,0:T(4,128)(2,1)S(1)}, bf16[1,3,512]{2,1,0:T(4,128)(2,1)S(1)}, u32[]{:S(2)}, u32[]{:S(2)}) collective-permute-start(bf16[1,3,512]{2,1,0:T(4,128)(2,1)S(1)} %pad_maximum_fusion.4), channel_id=1, source_target_pairs={{0,4},{4,8},{8,12},{12,16},{16,20},{20,24},{24,28},{1,5},{5,9},{9,... | collective-permute-start | bytes 9224 | tf_op jit(solution)/shard_map/ppermute | solution.py:16
  29.5 1.9 %collective-permute-start.11 = (bf16[1,3,512]{2,1,0:T(4,128)(2,1)S(1)}, bf16[1,3,512]{2,1,0:T(4,128)(2,1)S(1)}, u32[]{:S(2)}, u32[]{:S(2)}) collective-permute-start(bf16[1,3,512]{2,1,0:T(4,128)(2,1)S(1)} %pad_maximum_fusion.4), channel_id=1, source_target_pairs={{4,0},{8,4},{12,8},{16,12},{20,16},{24,20},{28,24},{5,1},{9,5},{13... | collective-permute-start | bytes 9224 | tf_op jit(solution)/shard_map/ppermute | solution.py:19
  31.5 0.7 pad_maximum_fusion.1
  32.2 0.6 gather_fusion.1
  32.8 1.6 %collective-permute-done.11 = bf16[1,3,512]{2,1,0:T(4,128)(2,1)S(1)} collective-permute-done((bf16[1,3,512]{2,1,0:T(4,128)(2,1)S(1)}, bf16[1,3,512]{2,1,0:T(4,128)(2,1)S(1)}, u32[]{:S(2)}, u32[]{:S(2)}) %collective-permute-start.11) | collective-permute-done | bytes 3104 | tf_op jit(solution)/shard_map/ppermute | solution.py:19
  34.4 0.7 pad_maximum_fusion.2
  35.2 0.6 gather_fusion.2
  35.8 1.0 %constant_dynamic-update-slice_fusion.1 = bf16[1,3,512,256]{3,2,1,0:T(8,128)(2,1)S(1)} fusion(bf16[1,3,512,256]{3,2,1,0:T(8,128)(2,1)S(1)} %constant_dynamic-update-slice_fusion.2, bf16[1,1,512,256]{3,2,1,0:T(8,128)(2,1)} %param.7), kind=kLoop, calls=%fused_computation.63 | loop fusion | bytes 524288
  36.9 2.0 %collective-permute-start.2 = (bf16[1,3,512,256]{3,2,1,0:T(8,128)(2,1)S(1)}, bf16[1,3,512,256]{3,2,1,0:T(8,128)(2,1)S(1)}, u32[]{:S(2)}, u32[]{:S(2)}) collective-permute-start(bf16[1,3,512,256]{3,2,1,0:T(8,128)(2,1)S(1)} %constant_dynamic-update-slice_fusion), channel_id=1, source_target_pairs={{0,4},{4,8},{8,12},{12,16},{16,20},{20,24},{24,28},{1,5},{5,9},{9,... | collective-permute-start | bytes 2359304 | tf_op jit(solution)/shard_map/ppermute | solution.py:16
  38.9 2.3 %collective-permute-start.3 = (bf16[1,3,512,256]{3,2,1,0:T(8,128)(2,1)S(1)}, bf16[1,3,512,256]{3,2,1,0:T(8,128)(2,1)S(1)}, u32[]{:S(2)}, u32[]{:S(2)}) collective-permute-start(bf16[1,3,512,256]{3,2,1,0:T(8,128)(2,1)S(1)} %constant_dynamic-update-slice_fusion), channel_id=1, source_target_pairs={{4,0},{8,4},{12,8},{16,12},{20,16},{24,20},{28,24},{5,1},{9,5},{13... | collective-permute-start | bytes 2359304 | tf_op jit(solution)/shard_map/ppermute | solution.py:19
  42.0 5.9 %collective-permute-done.2 = bf16[1,3,512,256]{3,2,1,0:T(8,128)(2,1)S(1)} collective-permute-done((bf16[1,3,512,256]{3,2,1,0:T(8,128)(2,1)S(1)}, bf16[1,3,512,256]{3,2,1,0:T(8,128)(2,1)S(1)}, u32[]{:S(2)}, u32[]{:S(2)}) %collective-permute-start.2) | collective-permute-done | bytes 786464 | tf_op jit(solution)/shard_map/ppermute | solution.py:16
  47.8 4.4 %collective-permute-done.3 = bf16[1,3,512,256]{3,2,1,0:T(8,128)(2,1)S(1)} collective-permute-done((bf16[1,3,512,256]{3,2,1,0:T(8,128)(2,1)S(1)}, bf16[1,3,512,256]{3,2,1,0:T(8,128)(2,1)S(1)}, u32[]{:S(2)}, u32[]{:S(2)}) %collective-permute-start.3) | collective-permute-done | bytes 786464 | tf_op jit(solution)/shard_map/ppermute | solution.py:19
  52.2 1.7 %pad_maximum_fusion = bf16[3,3,512,256]{3,2,1,0:T(8,128)(2,1)} fusion(bf16[1,3,512,256]{3,2,1,0:T(8,128)(2,1)S(1)} %collective-permute-done.3, bf16[1,3,512,256]{3,2,1,0:T(8,128)(2,1)S(1)} %constant_dynamic-update-slice_fusion, bf16[1,3,512,256]{3,2,1,0:T(8,128)(2,1)S(1)} %collective-permute-done.2), kind=kLoop, calls=%fused_computation.7 | loop fusion | flops 2359296 | bytes 4718592 | tf_op jit(solution)/shard_map/concatenate | solution.py:20
  53.9 2.4 %gather_fusion = bf16[9,512,256]{2,1,0:T(8,128)(2,1)S(1)} fusion(bf16[9,512,256]{2,1,0:T(8,128)(2,1)} %bitcast.147, s32[1024]{0:T(1024)S(1)} %pad_clamp_fusion), kind=kCustom, calls=%fused_computation | custom fusion | bytes 4718628 | tf_op jit(solution)/shard_map/gather | solution.py:88
  56.2 2.2 %multiply_reduce_fusion = (f32[]{:T(128)}, f32[256,256]{1,0:T(8,128)S(1)}) fusion(bf16[9,512,256]{2,1,0:T(8,128)(2,1)S(1)} %gather_fusion, f32[9,512]{1,0:T(8,128)S(1)} %convert_multiply_fusion.1), kind=kOutput, calls=%fused_computation.46 | convolution fusion | flops 607846400 | bytes 2639876 | tf_op jit(solution)/shard_map/dot_general | solution.py:92
  59.4 0.4 fusion.18
  60.1 0.4 select_subtract_fusion.10
  60.5 0.4 fusion.28
  60.9 0.4 fusion.27
  61.3 0.4 select_subtract_fusion.9
  61.7 0.4 fusion.30
  62.1 0.4 fusion.29
  62.4 0.4 select_subtract_fusion.8
  62.8 0.4 fusion.32
  63.2 0.4 fusion.31
  63.6 0.4 select_subtract_fusion.7
  64.0 0.4 fusion.34
  64.4 0.4 fusion.33
  64.8 0.4 select_subtract_fusion.6
  65.2 0.4 fusion.36
  65.6 0.4 fusion.35
  65.9 0.4 select_subtract_fusion.5
  66.7 0.4 fusion.37
  67.1 0.4 select_subtract_fusion.4
  67.5 0.4 fusion.40
  67.9 0.4 fusion.39
  68.3 0.4 select_subtract_fusion.3
  69.0 0.6 fusion.41
  69.6 0.4 select_subtract_fusion.2
  70.0 0.4 fusion.44
  70.4 0.4 fusion.43
  70.8 0.4 select_subtract_fusion.1
  71.2 0.4 fusion.46
  71.5 0.4 fusion.45
  71.9 0.4 select_subtract_fusion
  72.3 0.4 fusion.47
  72.7 0.4 convolution_bitcast_fusion.1
  74.2 0.5 broadcast.213
  74.7 0.8 reduce.6
  75.7 12.2 %all_to_all.27 = bf16[8,2,8192]{2,1,0:T(2,128)(2,1)S(1)} all-to-all(bf16[8,2,8192]{2,1,0:T(2,128)(2,1)S(1)} %reshape.557), channel_id=1, replica_groups=mesh['mem'=8,'pat'=4] {'mem'}, dimensions={0} | all-to-all | bytes 524288 | tf_op jit(solution)/shard_map/all_to_all | solution.py:106
  88.3 0.9 copy.28
  (34 shorter events, 4.0 us)
Async XLA Ops:
  0.0 16.0 %collective-permute-start.4 = (bf16[1,1,512]{2,1,0:T(2,128)(2,1)}, bf16[1,1,512]{2,1,0:T(2,128)(2,1)S(1)}, u32[]{:S(2)}, u32[]{:S(2)}) collective-permute-start(bf16[1,1,512]{2,1,0:T(2,128)(2,1)} %param.9), channel_id=1, source_target_pairs={{0,1},{1,2},{2,3},{3,0},{4,5},{5,6},{6,7},{7,4},{8,9},{9,10},{10,1... | collective-permute-start | bytes 3080 | tf_op jit(solution)/shard_map/ppermute | solution.py:16
  2.0 16.6 %collective-permute-start.5 = (bf16[1,1,512]{2,1,0:T(2,128)(2,1)}, bf16[1,1,512]{2,1,0:T(2,128)(2,1)S(1)}, u32[]{:S(2)}, u32[]{:S(2)}) collective-permute-start(bf16[1,1,512]{2,1,0:T(2,128)(2,1)} %param.9), channel_id=1, source_target_pairs={{1,0},{2,1},{3,2},{0,3},{5,4},{6,5},{7,6},{4,7},{9,8},{10,9},{11,1... | collective-permute-start | bytes 3080 | tf_op jit(solution)/shard_map/ppermute | solution.py:19
  3.0 32.8 %collective-permute-start = (bf16[1,1,512,256]{3,2,1,0:T(8,128)(2,1)}, bf16[1,1,512,256]{3,2,1,0:T(8,128)(2,1)S(1)}, u32[]{:S(2)}, u32[]{:S(2)}) collective-permute-start(bf16[1,1,512,256]{3,2,1,0:T(8,128)(2,1)} %param.7), channel_id=1, source_target_pairs={{0,1},{1,2},{2,3},{3,0},{4,5},{5,6},{6,7},{7,4},{8,9},{9,10},{10,1... | collective-permute-start | bytes 786440 | tf_op jit(solution)/shard_map/ppermute | solution.py:16
  3.5 33.3 %collective-permute-start.1 = (bf16[1,1,512,256]{3,2,1,0:T(8,128)(2,1)}, bf16[1,1,512,256]{3,2,1,0:T(8,128)(2,1)S(1)}, u32[]{:S(2)}, u32[]{:S(2)}) collective-permute-start(bf16[1,1,512,256]{3,2,1,0:T(8,128)(2,1)} %param.7), channel_id=1, source_target_pairs={{1,0},{2,1},{3,2},{0,3},{5,4},{6,5},{7,6},{4,7},{9,8},{10,9},{11,1... | collective-permute-start | bytes 786440 | tf_op jit(solution)/shard_map/ppermute | solution.py:19
  5.4 17.9 %collective-permute-start.8 = (bf16[1,1,512]{2,1,0:T(2,128)(2,1)}, bf16[1,1,512]{2,1,0:T(2,128)(2,1)S(1)}, u32[]{:S(2)}, u32[]{:S(2)}) collective-permute-start(bf16[1,1,512]{2,1,0:T(2,128)(2,1)} %param.8), channel_id=1, source_target_pairs={{0,1},{1,2},{2,3},{3,0},{4,5},{5,6},{6,7},{7,4},{8,9},{9,10},{10,1... | collective-permute-start | bytes 3080 | tf_op jit(solution)/shard_map/ppermute | solution.py:16
  7.3 33.9 %all-to-all-start = ((bf16[32,8,1,512]{3,0,2,1:T(8,128)(2,1)}), bf16[32,8,1,512]{3,0,2,1:T(8,128)(2,1)S(1)}, u32[]{:S(2)}, u32[]{:S(2)}) async-start(bf16[32,8,1,512]{3,0,2,1:T(8,128)(2,1)} %copy.23), calls=%async_computation | async-start | bytes 524288 | tf_op jit(solution)/shard_map/all_to_all | solution.py:55
  16.0 9.1 %collective-permute-start.9 = (bf16[1,1,512]{2,1,0:T(2,128)(2,1)}, bf16[1,1,512]{2,1,0:T(2,128)(2,1)S(1)}, u32[]{:S(2)}, u32[]{:S(2)}) collective-permute-start(bf16[1,1,512]{2,1,0:T(2,128)(2,1)} %param.8), channel_id=1, source_target_pairs={{1,0},{2,1},{3,2},{0,3},{5,4},{6,5},{7,6},{4,7},{9,8},{10,9},{11,1... | collective-permute-start | bytes 3080 | tf_op jit(solution)/shard_map/ppermute | solution.py:19
  19.4 10.1 %collective-permute-start.6 = (bf16[1,3,512]{2,1,0:T(4,128)(2,1)S(1)}, bf16[1,3,512]{2,1,0:T(4,128)(2,1)S(1)}, u32[]{:S(2)}, u32[]{:S(2)}) collective-permute-start(bf16[1,3,512]{2,1,0:T(4,128)(2,1)S(1)} %pad_maximum_fusion.3), channel_id=1, source_target_pairs={{0,4},{4,8},{8,12},{12,16},{16,20},{20,24},{24,28},{1,5},{5,9},{9,... | collective-permute-start | bytes 9224 | tf_op jit(solution)/shard_map/ppermute | solution.py:16
  23.2 8.2 %collective-permute-start.7 = (bf16[1,3,512]{2,1,0:T(4,128)(2,1)S(1)}, bf16[1,3,512]{2,1,0:T(4,128)(2,1)S(1)}, u32[]{:S(2)}, u32[]{:S(2)}) collective-permute-start(bf16[1,3,512]{2,1,0:T(4,128)(2,1)S(1)} %pad_maximum_fusion.3), channel_id=1, source_target_pairs={{4,0},{8,4},{12,8},{16,12},{20,16},{24,20},{28,24},{5,1},{9,5},{13... | collective-permute-start | bytes 9224 | tf_op jit(solution)/shard_map/ppermute | solution.py:19
  25.9 7.0 %collective-permute-start.10 = (bf16[1,3,512]{2,1,0:T(4,128)(2,1)S(1)}, bf16[1,3,512]{2,1,0:T(4,128)(2,1)S(1)}, u32[]{:S(2)}, u32[]{:S(2)}) collective-permute-start(bf16[1,3,512]{2,1,0:T(4,128)(2,1)S(1)} %pad_maximum_fusion.4), channel_id=1, source_target_pairs={{0,4},{4,8},{8,12},{12,16},{16,20},{20,24},{24,28},{1,5},{5,9},{9,... | collective-permute-start | bytes 9224 | tf_op jit(solution)/shard_map/ppermute | solution.py:16
  29.5 4.9 %collective-permute-start.11 = (bf16[1,3,512]{2,1,0:T(4,128)(2,1)S(1)}, bf16[1,3,512]{2,1,0:T(4,128)(2,1)S(1)}, u32[]{:S(2)}, u32[]{:S(2)}) collective-permute-start(bf16[1,3,512]{2,1,0:T(4,128)(2,1)S(1)} %pad_maximum_fusion.4), channel_id=1, source_target_pairs={{4,0},{8,4},{12,8},{16,12},{20,16},{24,20},{28,24},{5,1},{9,5},{13... | collective-permute-start | bytes 9224 | tf_op jit(solution)/shard_map/ppermute | solution.py:19
  36.9 11.0 %collective-permute-start.2 = (bf16[1,3,512,256]{3,2,1,0:T(8,128)(2,1)S(1)}, bf16[1,3,512,256]{3,2,1,0:T(8,128)(2,1)S(1)}, u32[]{:S(2)}, u32[]{:S(2)}) collective-permute-start(bf16[1,3,512,256]{3,2,1,0:T(8,128)(2,1)S(1)} %constant_dynamic-update-slice_fusion), channel_id=1, source_target_pairs={{0,4},{4,8},{8,12},{12,16},{16,20},{20,24},{24,28},{1,5},{5,9},{9,... | collective-permute-start | bytes 2359304 | tf_op jit(solution)/shard_map/ppermute | solution.py:16
  38.9 13.3 %collective-permute-start.3 = (bf16[1,3,512,256]{3,2,1,0:T(8,128)(2,1)S(1)}, bf16[1,3,512,256]{3,2,1,0:T(8,128)(2,1)S(1)}, u32[]{:S(2)}, u32[]{:S(2)}) collective-permute-start(bf16[1,3,512,256]{3,2,1,0:T(8,128)(2,1)S(1)} %constant_dynamic-update-slice_fusion), channel_id=1, source_target_pairs={{4,0},{8,4},{12,8},{16,12},{20,16},{24,20},{28,24},{5,1},{9,5},{13... | collective-permute-start | bytes 2359304 | tf_op jit(solution)/shard_map/ppermute | solution.py:19
where the time goes:
time: 90.8 us; the launch traced here: 89.1 us
  starting transfers between devices  30.6 us (34%)
  matrix products  16.8 us (19%)
  blocking collectives  12.2 us (13%)
  waiting for transfers between devices  11.9 us (13%)
  local copies, waits for them, and re-layouts  8.45 us (9%)
  other arithmetic  7.13 us (8%)
  between operations  1.99 us (2%)
    ppermute x6, starting transfers between devices, padded(): lax.ppermute(lax.slice_in_dim(block, block.shape[dim] - width, None, axis...  12.3 us
    all_to_all x1, blocking collectives, on_device(): lax.all_to_all(analysed, 'mem', split_axis=0, concat_axis=1, tiled=True)  12.2 us
    ppermute x6, starting transfers between devices, padded(): lax.ppermute(lax.slice_in_dim(block, 0, width, axis=dim), axis, backward)  11.6 us
    all_to_all x1, starting transfers between devices, on_device(): lax.all_to_all(background_realisations, 'mem', split_axis=1, concat_axis=...  6.67 us
    ppermute x6, waiting for transfers between devices, padded(): lax.ppermute(lax.slice_in_dim(block, 0, width, axis=dim), axis, backward)  6.01 us
    ppermute x6, waiting for transfers between devices, padded(): lax.ppermute(lax.slice_in_dim(block, block.shape[dim] - width, None, axis...  5.88 us
    dot_general x12, matrix products, transform(): jnp.einsum('pij,pjk->pik', correction, inverse_root, precision=lax.Precis...  4.63 us
    dot_general x12, matrix products, transform(): jnp.einsum('pij,pjk->pik', inverse_root, iterate, precision=lax.Precision...  4.51 us
  transfers between devices with their start and end apart: 13, of which 3 were waited for; matrix products, arithmetic and copies ran while one was open for 10% of the time, Pallas kernels for 0%

commit v1 on v0

v1 whole, which is shorter than its diff:
```python
import functools

import jax
import jax.numpy as jnp
from jax import lax
from jax.experimental import pallas as pl
from jax.experimental.pallas import tpu as pltpu
from jax.sharding import PartitionSpec as P

ITERS = 12


def split(value):
    high = value.astype(jnp.bfloat16)
    low = (value - high.astype(jnp.float32)).astype(jnp.bfloat16)
    return high, low


def product(left, right):
    return jnp.dot(
        jnp.concatenate([left[1], left[0], left[0]], axis=1),
        jnp.concatenate([right[0], right[1], right[0]], axis=0),
        preferred_element_type=jnp.float32,
    )


def kernel(
    rows,
    cols,
    states_ref,
    spreads_ref,
    innov_ref,
    rinv_ref,
    labels_ref,
    length_ref,
    out_ref,
    forecast,
    grams,
    coefs,
    sums,
    arrived,
    total,
    y_high,
    y_low,
    z_high,
    z_low,
    anomaly,
    analysed,
    fsend,
    frecv,
    gsend,
    grecv,
    ysend,
    yrecv,
    csend,
    crecv,
    ssend,
    srecv,
    osend,
    orecv,
):
    row = lax.axis_index("mem")
    col = lax.axis_index("pat")
    odd = lax.rem(col, 2)
    partner = col + 1 - 2 * odd
    onward = lax.rem(col + 2 - 4 * odd + cols, cols)
    behind = lax.rem(col - 2 + 4 * odd + cols, cols)
    members = forecast.shape[0] * forecast.shape[1]
    half = members // 2
    chunks = ((0, half), (half, half), (2 * half, half + 8))

    barrier = pltpu.get_barrier_semaphore()
    greeted = 0
    for step in range(1, rows):
        pl.semaphore_signal(barrier, 1, device_id={"mem": lax.rem(row + step, rows)})
        greeted += 1
    pat_peers = [partner, onward] + ([behind] if cols > 4 else [])
    for peer in pat_peers:
        pl.semaphore_signal(barrier, 1, device_id={"pat": peer})
        greeted += 1

    slot = lax.broadcasted_iota(jnp.int32, (16, labels_ref.shape[2]), 1)
    code = lax.broadcasted_iota(jnp.int32, (16, labels_ref.shape[2]), 0)
    used = (labels_ref[0] == code) & (slot < length_ref[...])
    shift_row = code // 3 - 1
    shift_col = code % 3 - 1
    distance = (shift_row * shift_row + shift_col * shift_col).astype(jnp.float32)
    coefficient = jnp.sum(
        jnp.where(used, jnp.exp(-0.5 * distance), 0.0), axis=1, keepdims=True
    )
    coefs[1] = jnp.broadcast_to(coefficient, coefs.shape[1:])

    block = spreads_ref[...]
    weight = rinv_ref[0].astype(jnp.float32)
    scaled = jnp.concatenate(split(block.astype(jnp.float32).T * weight), axis=1)
    twice = jnp.concatenate([block, block], axis=0)
    upper = jnp.dot(scaled[:half], twice, preferred_element_type=jnp.float32)
    lower = jnp.dot(scaled[half:], twice[:, half:], preferred_element_type=jnp.float32)
    grams[0, 0:half] = upper[:, :half]
    grams[0, half : 2 * half] = upper[:, half:]
    grams[0, 2 * half : 3 * half] = lower
    weighted = split(weight * innov_ref[0].astype(jnp.float32))
    drive = jnp.dot(
        jnp.broadcast_to(jnp.concatenate(weighted, axis=1), (16, 2 * weight.shape[1])),
        twice,
        preferred_element_type=jnp.float32,
    )
    grams[0, 3 * half : 3 * half + 8] = jnp.concatenate(
        [drive[0:4, :half], drive[0:4, half:]], axis=0
    )
    pl.semaphore_wait(barrier, greeted)

    def across(part):
        start, size = chunks[part]
        return pltpu.make_async_remote_copy(
            src_ref=grams.at[0, pl.ds(start, size)],
            dst_ref=grams.at[1, pl.ds(start, size)],
            send_sem=gsend.at[part],
            recv_sem=grecv.at[part],
            device_id={"pat": partner},
        )

    def relay(part):
        start, size = chunks[part]
        return pltpu.make_async_remote_copy(
            src_ref=grams.at[1, pl.ds(start, size)],
            dst_ref=grams.at[2, pl.ds(start, size)],
            send_sem=ysend.at[part],
            recv_sem=yrecv.at[part],
            device_id={"pat": onward},
        )

    def coef_copy(up):
        return pltpu.make_async_remote_copy(
            src_ref=coefs.at[1],
            dst_ref=coefs.at[0 if up else 2],
            send_sem=csend.at[0 if up else 1],
            recv_sem=crecv.at[0 if up else 1],
            device_id={"mem": row + 1 if up else row - 1},
        )

    def sum_copy(up, part):
        start, size = chunks[part]
        side = 0 if up else 1
        return pltpu.make_async_remote_copy(
            src_ref=sums.at[side, pl.ds(start, size)],
            dst_ref=arrived.at[side, pl.ds(start, size)],
            send_sem=ssend.at[side, part],
            recv_sem=srecv.at[side, part],
            device_id={"mem": row + 1 if up else row - 1},
        )

    def forecast_copy(step):
        peer = lax.rem(row + step, rows)
        return pltpu.make_async_remote_copy(
            src_ref=states_ref.at[peer],
            dst_ref=forecast.at[row],
            send_sem=fsend.at[step],
            recv_sem=frecv.at[step],
            device_id={"mem": peer},
        )

    def analysis_copy(step):
        peer = lax.rem(row + step, rows)
        return pltpu.make_async_remote_copy(
            src_ref=analysed.at[peer],
            dst_ref=out_ref.at[row],
            send_sem=osend.at[step],
            recv_sem=orecv.at[step],
            device_id={"mem": peer},
        )

    for part in range(3):
        across(part).start()

    @pl.when(row < rows - 1)
    def _():
        coef_copy(True).start()

    @pl.when(row > 0)
    def _():
        coef_copy(False).start()

    for step in range(1, rows):
        forecast_copy(step).start()
    forecast[row] = states_ref[row]

    for part in range(3):
        across(part).wait_recv()
        relay(part).start()

    @pl.when(row > 0)
    def _():
        coef_copy(True).wait_recv()

    @pl.when(row < rows - 1)
    def _():
        coef_copy(False).wait_recv()

    def combined(target, first, start, size):
        own = coefs[target, pl.ds(first + 1, 1), :]
        near = coefs[target, pl.ds(first + 2 - 2 * odd, 1), :]
        far = coefs[target, pl.ds(first + 2 * odd, 1), :]
        piece = pl.ds(start, size)
        return own * grams[0, piece] + near * grams[1, piece] + far * grams[2, piece]

    for part in range(3):
        relay(part).wait_recv()
        start, size = chunks[part]

        @pl.when(row < rows - 1)
        def _():
            sums[0, pl.ds(start, size)] = combined(2, 0, start, size)
            sum_copy(True, part).start()

        @pl.when(row > 0)
        def _():
            sums[1, pl.ds(start, size)] = combined(0, 6, start, size)
            sum_copy(False, part).start()

        total[pl.ds(start, size)] = combined(1, 3, start, size)

    for step in range(1, rows):
        forecast_copy(step).wait_recv()
    values = forecast[...].reshape(members, forecast.shape[2]).astype(jnp.float32)
    center = jnp.sum(values, axis=0, keepdims=True) * (1.0 / members)
    anomaly[...] = (values - center).astype(jnp.bfloat16)

    for part in range(3):
        start, size = chunks[part]

        @pl.when(row > 0)
        def _():
            sum_copy(True, part).wait_recv()
            total[pl.ds(start, size)] += arrived[0, pl.ds(start, size)]

        @pl.when(row < rows - 1)
        def _():
            sum_copy(False, part).wait_recv()
            total[pl.ds(start, size)] += arrived[1, pl.ds(start, size)]

    eye_half = (
        lax.broadcasted_iota(jnp.int32, (half, half), 0)
        == lax.broadcasted_iota(jnp.int32, (half, half), 1)
    ).astype(jnp.float32)
    first = total[0:half] + (members - 1.0) * eye_half
    cross = total[half : 2 * half]
    last = total[2 * half : 3 * half] + (members - 1.0) * eye_half
    squares = first * first + 2.0 * (cross * cross) + last * last
    frobenius = jnp.sqrt(
        jnp.sum(jnp.sum(squares, axis=0, keepdims=True), axis=1, keepdims=True)
    )
    system = jnp.concatenate(
        [
            jnp.concatenate([first, cross], axis=1),
            jnp.concatenate([cross.T, last], axis=1),
        ],
        axis=0,
    )
    identity = (
        lax.broadcasted_iota(jnp.int32, (members, members), 0)
        == lax.broadcasted_iota(jnp.int32, (members, members), 1)
    ).astype(jnp.float32)
    iterate = system / frobenius
    correction = split(1.5 * identity - 0.5 * iterate)
    z_high[...], z_low[...] = correction
    y_high[...], y_low[...] = split(product(split(iterate), correction))

    def sweep(index, carry):
        y = (y_high[...], y_low[...])
        z = (z_high[...], z_low[...])
        correction = split(1.5 * identity - 0.5 * product(z, y))
        y_high[...], y_low[...] = split(product(y, correction))
        z_high[...], z_low[...] = split(product(correction, z))
        return carry

    lax.fori_loop(1, ITERS - 1, sweep, 0)
    z = (z_high[...], z_low[...])
    correction = split(1.5 * identity - 0.5 * product(z, (y_high[...], y_low[...])))
    inverse_root = product(correction, z)
    root = split(inverse_root)
    driven = jnp.concatenate(
        [
            jnp.broadcast_to(total[3 * half : 3 * half + 1], (half, half)).T,
            jnp.broadcast_to(total[3 * half + 4 : 3 * half + 5], (half, half)).T,
        ],
        axis=0,
    )
    inner = product(root, split(driven))
    mean = product(root, split(inner)) / frobenius
    mixing = (
        inverse_root * jnp.sqrt((members - 1.0) / frobenius)
        + jnp.concatenate([mean, mean], axis=1)
    ).astype(jnp.bfloat16)
    mixed = lax.dot_general(
        mixing, anomaly[...], (((0,), (0,)), ((), ())), preferred_element_type=jnp.float32
    )
    analysed[...] = (center + mixed).astype(jnp.bfloat16).reshape(analysed.shape)
    for step in range(1, rows):
        analysis_copy(step).start()
    out_ref[row] = analysed[row]

    for part in range(3):
        across(part).wait_send()
        relay(part).wait_send()

    @pl.when(row < rows - 1)
    def _():
        coef_copy(True).wait_send()
        for part in range(3):
            sum_copy(True, part).wait_send()

    @pl.when(row > 0)
    def _():
        coef_copy(False).wait_send()
        for part in range(3):
            sum_copy(False, part).wait_send()

    for step in range(1, rows):
        forecast_copy(step).wait_send()
    for step in range(1, rows):
        analysis_copy(step).wait()


def solution(mesh):
    rows, cols = mesh.shape["mem"], mesh.shape["pat"]

    def on_device(states, spreads, innov, rinv, labels, lengths):
        share, _, _, state_len = states.shape
        obs, members = spreads.shape[2:]
        packed = 3 * (members // 2) + 8
        by_row = jnp.transpose(states.reshape(share, rows, state_len), (1, 0, 2))
        vmem = pl.BlockSpec(memory_space=pltpu.VMEM)
        dma = pltpu.SemaphoreType.DMA
        half = members // 2
        square = pltpu.VMEM((members, members), jnp.bfloat16)
        out = pl.pallas_call(
            functools.partial(kernel, rows, cols),
            out_shape=jax.ShapeDtypeStruct((rows, share, state_len), jnp.bfloat16),
            in_specs=[vmem] * 6,
            out_specs=vmem,
            scratch_shapes=[
                pltpu.VMEM((rows, share, state_len), jnp.bfloat16),
                pltpu.VMEM((3, packed, half), jnp.float32),
                pltpu.VMEM((3, 16, half), jnp.float32),
                pltpu.VMEM((2, packed, half), jnp.float32),
                pltpu.VMEM((2, packed, half), jnp.float32),
                pltpu.VMEM((packed, half), jnp.float32),
                square,
                square,
                square,
                square,
                pltpu.VMEM((members, state_len), jnp.bfloat16),
                pltpu.VMEM((rows, share, state_len), jnp.bfloat16),
                dma((rows,)),
                dma((rows,)),
                dma((3,)),
                dma((3,)),
                dma((3,)),
                dma((3,)),
                dma((2,)),
                dma((2,)),
                dma((2, 3)),
                dma((2, 3)),
                dma((rows,)),
                dma((rows,)),
            ],
            compiler_params=pltpu.CompilerParams(collective_id=0, has_side_effects=True),
        )(
            by_row,
            spreads.reshape(obs, members),
            innov.reshape(1, 1, obs),
            rinv.reshape(1, 1, obs),
            labels,
            lengths,
        )
        return jnp.transpose(out, (1, 0, 2)).reshape(states.shape)

    placed = (
        P("mem", None, "pat", None),
        P("mem", "pat", None, None),
        P("mem", "pat", None),
        P("mem", "pat", None),
        P("mem", "pat", None),
        P("mem", "pat"),
    )
    return jax.shard_map(
        on_device,
        mesh=mesh,
        in_specs=placed,
        out_specs=P("mem", None, "pat", None),
        check_vma=False,
    )
```

time: 90.8 us -> 37.2 us (0.41); the launches traced: 89.1 us -> 37 us
  Pallas kernels: 0 us -> 32.8 us
  starting transfers between devices: 30.6 us -> 0 us
  matrix products: 16.8 us -> 0 us
  blocking collectives: 12.2 us -> 0 us
  waiting for transfers between devices: 11.9 us -> 0 us
  other arithmetic: 7.13 us -> 0 us
  local copies, waits for them, and re-layouts: 8.45 us -> 3.53 us
  between operations: 1.99 us -> 0.66 us
    pallas_call x0 -> x1, Pallas kernels: none -> 32.8 us  [on_device(): pl.pallas_call(functools.partial(kernel, rows, cols), out_shape=jax.Shape...]
    ppermute x12 -> x0, starting transfers between devices: 23.9 us -> none  [the longest x6 12.3 us: padded(): lax.ppermute(lax.slice_in_dim(block, block.shape[dim] - width, None, axis...]
    dot_general x40 -> x0, matrix products: 16.8 us -> none  [the longest x12 4.63 us: transform(): jnp.einsum('pij,pjk->pik', correction, inverse_root, precision=lax.Precis...]
    all_to_all x1 -> x0, blocking collectives: 12.2 us -> none  [on_device(): lax.all_to_all(analysed, 'mem', split_axis=0, concat_axis=1, tiled=True)]
    ppermute x12 -> x0, waiting for transfers between devices: 11.9 us -> none  [the longest x6 6.01 us: padded(): lax.ppermute(lax.slice_in_dim(block, 0, width, axis=dim), axis, backward)]
    all_to_all x1 -> x0, starting transfers between devices: 6.67 us -> none  [on_device(): lax.all_to_all(background_realisations, 'mem', split_axis=1, concat_axis=...]
    concatenate x5 -> x0, other arithmetic: 4.45 us -> none  [padded(): block = jnp.concatenate([low, block, high], axis=dim)]
    gather x3 -> x0, local copies, waits for them, and re-layouts: 3.51 us -> none  [the longest x1 2.36 us: on_device(): blocks = flat_ens[source]]
  transfers between devices with their start and end apart: 13 -> 0, of which waited for: 3 -> 0; matrix products, arithmetic and copies ran while one was open for 10% -> 0% of each run, Pallas kernels for 0% -> 0%
where the time goes in v1:
time: 37.2 us; the launch traced here: 37 us
  Pallas kernels  32.8 us (88%)
  local copies, waits for them, and re-layouts  3.53 us (9%)
  between operations  0.66 us (2%)
    pallas_call x1, Pallas kernels, on_device(): pl.pallas_call(functools.partial(kernel, rows, cols), out_shape=jax.Shape...  32.8 us
    reshape x1, local copies, waits for them, and re-layouts, on_device(): return jnp.transpose(out, (1, 0, 2)).reshape(states.shape)  1.8 us
    unnamed x1, local copies, waits for them, and re-layouts  1.73 us

profile of v1, /device:TPU:1, one launch (start us, length us, event | category | flops | bytes accessed | tf_op | source)
XLA Modules:
  0.0 37.0 jit_solution(12486712744233600261)
XLA Ops:
  0.7 1.7 %copy.10 = bf16[32,8,1,512]{3,0,1,2:T(8,128)(2,1)} copy(bf16[32,8,1,512]{3,1,2,0:T(8,128)(2,1)} %param.6) | data formatting | bytes 524288 | tf_op args[0]
  2.4 32.8 %shard_map.64 = bf16[8,32,512]{2,1,0:T(8,128)(2,1)} custom-call(bf16[8,32,512]{2,1,0:T(8,128)(2,1)} %bitcast.10, bf16[512,256]{1,0:T(8,128)(2,1)} %bitcast.11, bf16[1,1,512]{2,1,0:T(2,128)(2,1)} %innov_ref.1, bf16[1,1,512]{2,1,0:T(2,128)(2,1)} %rinv_ref.1, s32[1,1,9]{2,1,0:T(1,128)} %labels_ref.1, s32[1,1]{1,0:T(1,128)S(6)} %copy.11.length_ref), custom_call_target="tpu_custom_call" | custom-call | tf_op jit(solution)/shard_map/pallas_call | solution.py:337
  35.2 1.8 %copy.8 = bf16[32,8,1,512]{3,1,2,0:T(8,128)(2,1)} copy(bf16[32,8,1,512]{3,0,1,2:T(8,128)(2,1)} %bitcast.9) | data formatting | bytes 524288 | tf_op jit(solution)/shard_map/reshape | solution.py:377

commit v2 on v1

--- a/solution.py
+++ b/solution.py
@@ -24,16 +24,42 @@
     )
 
 
+def left_product(left, right):
+    return jnp.dot(
+        jnp.concatenate(left, axis=1),
+        jnp.concatenate([right.astype(jnp.bfloat16)] * 2, axis=0),
+        preferred_element_type=jnp.float32,
+    )
+
+
+def right_product(left, right):
+    return jnp.dot(
+        jnp.concatenate([left.astype(jnp.bfloat16)] * 2, axis=1),
+        jnp.concatenate(right, axis=0),
+        preferred_element_type=jnp.float32,
+    )
+
+
+def store(full, high, low, value):
+    full[...] = value
+    high[...], low[...] = split(value)
+
+
 def kernel(
     rows,
     cols,
-    states_ref,
-    spreads_ref,
+    states_hbm,
+    spreads_hbm,
     innov_ref,
     rinv_ref,
     labels_ref,
     length_ref,
     out_ref,
+    states,
+    spreads_ref,
+    widened,
+    states_ref,
+    gathered,
     forecast,
     grams,
     coefs,
@@ -44,6 +70,8 @@
     y_low,
     z_high,
     z_low,
+    y_full,
+    z_full,
     anomaly,
     analysed,
     fsend,
@@ -58,6 +86,7 @@
     srecv,
     osend,
     orecv,
+    local,
 ):
     row = lax.axis_index("mem")
     col = lax.axis_index("pat")
@@ -67,17 +96,25 @@
     behind = lax.rem(col - 2 + 4 * odd + cols, cols)
     members = forecast.shape[0] * forecast.shape[1]
     half = members // 2
-    chunks = ((0, half), (half, half), (2 * half, half + 8))
+    step_rows = half // 2
+    chunks = tuple(
+        (start, step_rows + (8 if start == 3 * half - step_rows else 0))
+        for start in range(0, 3 * half, step_rows)
+    )
+    parts = len(chunks)
 
     barrier = pltpu.get_barrier_semaphore()
-    greeted = 0
-    for step in range(1, rows):
-        pl.semaphore_signal(barrier, 1, device_id={"mem": lax.rem(row + step, rows)})
-        greeted += 1
     pat_peers = [partner, onward] + ([behind] if cols > 4 else [])
     for peer in pat_peers:
         pl.semaphore_signal(barrier, 1, device_id={"pat": peer})
-        greeted += 1
+
+    for step in range(1, rows):
+        pl.semaphore_signal(barrier, 1, device_id={"mem": lax.rem(row + step, rows)})
+
+    load_spreads = pltpu.make_async_copy(spreads_hbm, spreads_ref, local.at[0])
+    load_spreads.start()
+    load_states = pltpu.make_async_copy(states_hbm, states, local.at[1])
+    load_states.start()
 
     slot = lax.broadcasted_iota(jnp.int32, (16, labels_ref.shape[2]), 1)
     code = lax.broadcasted_iota(jnp.int32, (16, labels_ref.shape[2]), 0)
@@ -90,6 +127,7 @@
     )
     coefs[1] = jnp.broadcast_to(coefficient, coefs.shape[1:])
 
+    load_spreads.wait()
     block = spreads_ref[...]
     weight = rinv_ref[0].astype(jnp.float32)
     scaled = jnp.concatenate(split(block.astype(jnp.float32).T * weight), axis=1)
@@ -108,7 +146,7 @@
     grams[0, 3 * half : 3 * half + 8] = jnp.concatenate(
         [drive[0:4, :half], drive[0:4, half:]], axis=0
     )
-    pl.semaphore_wait(barrier, greeted)
+    pl.semaphore_wait(barrier, len(pat_peers) + rows - 1)
 
     def across(part):
         start, size = chunks[part]
@@ -164,13 +202,13 @@
         peer = lax.rem(row + step, rows)
         return pltpu.make_async_remote_copy(
             src_ref=analysed.at[peer],
-            dst_ref=out_ref.at[row],
+            dst_ref=gathered.at[row],
             send_sem=osend.at[step],
             recv_sem=orecv.at[step],
             device_id={"mem": peer},
         )
 
-    for part in range(3):
+    for part in range(parts):
         across(part).start()
 
     @pl.when(row < rows - 1)
@@ -181,11 +219,23 @@
     def _():
         coef_copy(False).start()
 
+    load_states.wait()
+    share, state_len = states_ref.shape[1:]
+    lanes = widened.shape[2]
+    tiles = [slice(at, at + lanes) for at in range(0, state_len, lanes)]
+    for tile, where in enumerate(tiles):
+        wide = states[:, :, where].astype(jnp.float32)
+        widened[tile] = wide.reshape(widened.shape[1:])
+    for other in range(rows):
+        for tile, where in enumerate(tiles):
+            piece = widened[tile, pl.ds(other, share, stride=rows), :]
+            states_ref[other, :, where] = piece.astype(jnp.bfloat16)
+    forecast[row] = states_ref[row]
+
     for step in range(1, rows):
         forecast_copy(step).start()
-    forecast[row] = states_ref[row]
-
-    for part in range(3):
+
+    for part in range(parts):
         across(part).wait_recv()
         relay(part).start()
 
@@ -204,7 +254,7 @@
         piece = pl.ds(start, size)
         return own * grams[0, piece] + near * grams[1, piece] + far * grams[2, piece]
 
-    for part in range(3):
+    for part in range(parts):
         relay(part).wait_recv()
         start, size = chunks[part]
 
@@ -226,7 +276,7 @@
     center = jnp.sum(values, axis=0, keepdims=True) * (1.0 / members)
     anomaly[...] = (values - center).astype(jnp.bfloat16)
 
-    for part in range(3):
+    for part in range(parts):
         start, size = chunks[part]
 
         @pl.when(row > 0)
@@ -262,22 +312,29 @@
         == lax.broadcasted_iota(jnp.int32, (members, members), 1)
     ).astype(jnp.float32)
     iterate = system / frobenius
-    correction = split(1.5 * identity - 0.5 * iterate)
-    z_high[...], z_low[...] = correction
-    y_high[...], y_low[...] = split(product(split(iterate), correction))
-
-    def sweep(index, carry):
-        y = (y_high[...], y_low[...])
-        z = (z_high[...], z_low[...])
-        correction = split(1.5 * identity - 0.5 * product(z, y))
-        y_high[...], y_low[...] = split(product(y, correction))
-        z_high[...], z_low[...] = split(product(correction, z))
+    change = 0.5 * (identity - iterate)
+    store(z_full, z_high, z_low, identity + change)
+    store(y_full, y_high, y_low, iterate + left_product(split(iterate), change))
+
+    def sweep(exact, index, carry):
+        if exact:
+            near_identity = product((z_high[...], z_low[...]), (y_high[...], y_low[...]))
+        else:
+            near_identity = jnp.dot(
+                z_high[...], y_high[...], preferred_element_type=jnp.float32
+            )
+        change = 0.5 * (identity - near_identity)
+        y = y_full[...] + left_product((y_high[...], y_low[...]), change)
+        z = z_full[...] + right_product(change, (z_high[...], z_low[...]))
+        store(y_full, y_high, y_low, y)
+        store(z_full, z_high, z_low, z)
         return carry
 
-    lax.fori_loop(1, ITERS - 1, sweep, 0)
+    lax.fori_loop(1, ITERS - 3, functools.partial(sweep, False), 0)
+    lax.fori_loop(ITERS - 3, ITERS - 1, functools.partial(sweep, True), 0)
     z = (z_high[...], z_low[...])
-    correction = split(1.5 * identity - 0.5 * product(z, (y_high[...], y_low[...])))
-    inverse_root = product(correction, z)
+    change = 0.5 * (identity - product(z, (y_high[...], y_low[...])))
+    inverse_root = z_full[...] + right_product(change, z)
     root = split(inverse_root)
     driven = jnp.concatenate(
         [
@@ -298,28 +355,41 @@
     analysed[...] = (center + mixed).astype(jnp.bfloat16).reshape(analysed.shape)
     for step in range(1, rows):
         analysis_copy(step).start()
-    out_ref[row] = analysed[row]
-
-    for part in range(3):
+
+    def place(source, other):
+        wide = source.astype(jnp.float32)
+        for tile, where in enumerate(tiles):
+            widened[tile, pl.ds(other, share, stride=rows), :] = wide[:, where]
+
+    place(analysed[row], row)
+    for step in range(1, rows):
+        analysis_copy(step).wait_recv()
+        giver = lax.rem(row - step + rows, rows)
+        place(gathered[giver], giver)
+    for tile, where in enumerate(tiles):
+        shape = (share, rows, lanes)
+        out_ref[:, :, where] = widened[tile].reshape(shape).astype(jnp.bfloat16)
+
+    for part in range(parts):
         across(part).wait_send()
         relay(part).wait_send()
 
     @pl.when(row < rows - 1)
     def _():
         coef_copy(True).wait_send()
-        for part in range(3):
+        for part in range(parts):
             sum_copy(True, part).wait_send()
 
     @pl.when(row > 0)
     def _():
         coef_copy(False).wait_send()
-        for part in range(3):
+        for part in range(parts):
             sum_copy(False, part).wait_send()
 
     for step in range(1, rows):
         forecast_copy(step).wait_send()
     for step in range(1, rows):
-        analysis_copy(step).wait()
+        analysis_copy(step).wait_send()
 
 
 def solution(mesh):
@@ -329,17 +399,22 @@
         share, _, _, state_len = states.shape
         obs, members = spreads.shape[2:]
         packed = 3 * (members // 2) + 8
-        by_row = jnp.transpose(states.reshape(share, rows, state_len), (1, 0, 2))
+        parts = 6
         vmem = pl.BlockSpec(memory_space=pltpu.VMEM)
         dma = pltpu.SemaphoreType.DMA
         half = members // 2
         square = pltpu.VMEM((members, members), jnp.bfloat16)
         out = pl.pallas_call(
             functools.partial(kernel, rows, cols),
-            out_shape=jax.ShapeDtypeStruct((rows, share, state_len), jnp.bfloat16),
-            in_specs=[vmem] * 6,
+            out_shape=jax.ShapeDtypeStruct((share, rows, state_len), jnp.bfloat16),
+            in_specs=[pl.BlockSpec(memory_space=pl.ANY)] * 2 + [vmem] * 4,
             out_specs=vmem,
             scratch_shapes=[
+                pltpu.VMEM((share, rows, state_len), jnp.bfloat16),
+                pltpu.VMEM((obs, members), jnp.bfloat16),
+                pltpu.VMEM((state_len // half, share * rows, half), jnp.float32),
+                pltpu.VMEM((rows, share, state_len), jnp.bfloat16),
+                pltpu.VMEM((rows, share, state_len), jnp.bfloat16),
                 pltpu.VMEM((rows, share, state_len), jnp.bfloat16),
                 pltpu.VMEM((3, packed, half), jnp.float32),
                 pltpu.VMEM((3, 16, half), jnp.float32),
@@ -350,31 +425,34 @@
                 square,
                 square,
                 square,
+                pltpu.VMEM((members, members), jnp.float32),
+                pltpu.VMEM((members, members), jnp.float32),
                 pltpu.VMEM((members, state_len), jnp.bfloat16),
                 pltpu.VMEM((rows, share, state_len), jnp.bfloat16),
                 dma((rows,)),
                 dma((rows,)),
-                dma((3,)),
-                dma((3,)),
-                dma((3,)),
-                dma((3,)),
+                dma((parts,)),
+                dma((parts,)),
+                dma((parts,)),
+                dma((parts,)),
                 dma((2,)),
                 dma((2,)),
-                dma((2, 3)),
-                dma((2, 3)),
+                dma((2, parts)),
+                dma((2, parts)),
                 dma((rows,)),
                 dma((rows,)),
+                dma((2,)),
             ],
             compiler_params=pltpu.CompilerParams(collective_id=0, has_side_effects=True),
         )(
-            by_row,
+            states.reshape(share, rows, state_len),
             spreads.reshape(obs, members),
             innov.reshape(1, 1, obs),
             rinv.reshape(1, 1, obs),
             labels,
             lengths,
         )
-        return jnp.transpose(out, (1, 0, 2)).reshape(states.shape)
+        return out.reshape(states.shape)
 
     placed = (
         P("mem", None, "pat", None),

time: 37.2 us -> 33.8 us (0.909)
  local copies, waits for them, and re-layouts: 3.53 us -> 1.67 us
  Pallas kernels: 32.8 us -> 31.3 us
    reshape x1 -> x0, local copies, waits for them, and re-layouts: 1.8 us -> none  [on_device(): return jnp.transpose(out, (1, 0, 2)).reshape(states.shape)]
    pallas_call x1, Pallas kernels: 32.8 us -> 31.3 us  [on_device(): pl.pallas_call(functools.partial(kernel, rows, cols), out_shape=jax.Shape...]
where the time goes in v2:
time: 33.8 us; the launch traced here: 33.6 us
  Pallas kernels  31.3 us (93%)
  local copies, waits for them, and re-layouts  1.67 us (5%)
  between operations  0.66 us (2%)
    pallas_call x1, Pallas kernels, on_device(): pl.pallas_call(functools.partial(kernel, rows, cols), out_shape=jax.Shape...  31.3 us
    unnamed x1, local copies, waits for them, and re-layouts  1.67 us

profile of v2, /device:TPU:1, one launch (start us, length us, event | category | flops | bytes accessed | tf_op | source)
XLA Modules:
  0.0 33.6 jit_solution(13138058544976990208)
XLA Ops:
  0.7 31.3 %shard_map.64 = bf16[32,8,512]{2,1,0:T(8,128)(2,1)} custom-call(bf16[32,8,512]{2,1,0:T(8,128)(2,1)} %bitcast.6, bf16[512,256]{1,0:T(8,128)(2,1)} %bitcast.7, bf16[1,1,512]{2,1,0:T(2,128)(2,1)} %innov_ref.1, bf16[1,1,512]{2,1,0:T(2,128)(2,1)} %rinv_ref.1, s32[1,1,9]{2,1,0:T(1,128)} %labels_ref.1, s32[1,1]{1,0:T(1,128)S(6)} %copy.9.length_ref), custom_call_target="tpu_custom_call" | custom-call | tf_op jit(solution)/shard_map/pallas_call | solution.py:407
  32.0 1.7 %copy.10 = bf16[32,8,1,512]{3,1,2,0:T(8,128)(2,1)} copy(bf16[32,8,1,512]{3,1,2,0:T(8,128)(2,1)} %bitcast.5) | data formatting | bytes 524288

commit v3 on v2

--- a/solution.py
+++ b/solution.py
@@ -25,19 +25,21 @@
 
 
 def left_product(left, right):
-    return jnp.dot(
-        jnp.concatenate(left, axis=1),
-        jnp.concatenate([right.astype(jnp.bfloat16)] * 2, axis=0),
+    both = jnp.dot(
+        jnp.concatenate(left, axis=0),
+        right.astype(jnp.bfloat16),
         preferred_element_type=jnp.float32,
     )
+    return both[: right.shape[0]] + both[right.shape[0] :]
 
 
 def right_product(left, right):
-    return jnp.dot(
-        jnp.concatenate([left.astype(jnp.bfloat16)] * 2, axis=1),
-        jnp.concatenate(right, axis=0),
+    both = jnp.dot(
+        left.astype(jnp.bfloat16),
+        jnp.concatenate(right, axis=1),
         preferred_element_type=jnp.float32,
     )
+    return both[:, : left.shape[1]] + both[:, left.shape[1] :]
 
 
 def store(full, high, low, value):
@@ -316,13 +318,10 @@
     store(z_full, z_high, z_low, identity + change)
     store(y_full, y_high, y_low, iterate + left_product(split(iterate), change))
 
-    def sweep(exact, index, carry):
-        if exact:
-            near_identity = product((z_high[...], z_low[...]), (y_high[...], y_low[...]))
-        else:
-            near_identity = jnp.dot(
-                z_high[...], y_high[...], preferred_element_type=jnp.float32
-            )
+    def sweep(index, carry):
+        near_identity = jnp.dot(
+            z_high[...], y_high[...], preferred_element_type=jnp.float32
+        )
         change = 0.5 * (identity - near_identity)
         y = y_full[...] + left_product((y_high[...], y_low[...]), change)
         z = z_full[...] + right_product(change, (z_high[...], z_low[...]))
@@ -330,8 +329,7 @@
         store(z_full, z_high, z_low, z)
         return carry
 
-    lax.fori_loop(1, ITERS - 3, functools.partial(sweep, False), 0)
-    lax.fori_loop(ITERS - 3, ITERS - 1, functools.partial(sweep, True), 0)
+    lax.fori_loop(1, ITERS - 1, sweep, 0)
     z = (z_high[...], z_low[...])
     change = 0.5 * (identity - product(z, (y_high[...], y_low[...])))
     inverse_root = z_full[...] + right_product(change, z)

time: 33.8 us -> 33.3 us (0.985)
  Pallas kernels: 31.3 us -> 30.8 us
    pallas_call x1, Pallas kernels: 31.3 us -> 30.8 us  [on_device(): pl.pallas_call(functools.partial(kernel, rows, cols), out_shape=jax.Shape...]
where the time goes in v3:
time: 33.3 us; the launch traced here: 33.1 us
  Pallas kernels  30.8 us (92%)
  local copies, waits for them, and re-layouts  1.67 us (5%)
  between operations  0.66 us (2%)
    pallas_call x1, Pallas kernels, on_device(): pl.pallas_call(functools.partial(kernel, rows, cols), out_shape=jax.Shape...  30.8 us
    unnamed x1, local copies, waits for them, and re-layouts  1.67 us

profile of v3, /device:TPU:1, one launch (start us, length us, event | category | flops | bytes accessed | tf_op | source)
XLA Modules:
  0.0 33.1 jit_solution(403059502453418982)
XLA Ops:
  0.7 30.8 %shard_map.64 = bf16[32,8,512]{2,1,0:T(8,128)(2,1)} custom-call(bf16[32,8,512]{2,1,0:T(8,128)(2,1)} %bitcast.6, bf16[512,256]{1,0:T(8,128)(2,1)} %bitcast.7, bf16[1,1,512]{2,1,0:T(2,128)(2,1)} %innov_ref.1, bf16[1,1,512]{2,1,0:T(2,128)(2,1)} %rinv_ref.1, s32[1,1,9]{2,1,0:T(1,128)} %labels_ref.1, s32[1,1]{1,0:T(1,128)S(6)} %copy.9.length_ref), custom_call_target="tpu_custom_call" | custom-call | tf_op jit(solution)/shard_map/pallas_call | solution.py:405
  31.4 1.7 %copy.10 = bf16[32,8,1,512]{3,1,2,0:T(8,128)(2,1)} copy(bf16[32,8,1,512]{3,1,2,0:T(8,128)(2,1)} %bitcast.5) | data formatting | bytes 524288
